TPU v7x, 256 devices: a whole 4x4x8 slice. The times are simulated.
256 devices in a mesh: grp: 8 (over y, core), dev: 32 (over z, x).
Axes of the slice: x: 4, y: 4, z: 8, core: 2. Of those that a mesh axis runs over, the one named last changes fastest.
Arguments:
- item_factors: bfloat16 [65536, 256], P(('grp', 'dev'))
- send_list: int32 [256, 8, 1], P(('grp', 'dev')), may hold values from 0 to 1
- route_list: int32 [256, 32, 1], P(('grp', 'dev')), may hold values from 0 to 7
- tile_slot: int32 [256, 64], P(('grp', 'dev')), may hold values from 0 to 31
- confidence: bfloat16 [16384, 128, 128], P(('grp', 'dev')), may hold values from 0 to 160, as said below
Outputs:
- user_factors: float32 [131072, 256], P(('grp', 'dev'))
Inputs may be any that keep to these rules, and one draw needn't show every extreme that they name: `confidence`: every user row of every tile has at least one observed item.
All inputs are finite; a program needn't handle non-finite values.
Results may differ from a plain program's by a relative error of at most 0.0055.
Values may be sent and summed in bfloat16 or wider, within the bound.
A program may use at most 128 MiB of HBM per device.

v0:
```python
import jax
import jax.numpy as jnp
from jax import lax
from jax.sharding import PartitionSpec as P

RANK = 256
BLOCK = 128
PANELS_DEV = 2
USER_BLOCKS = 4
TILES_PER = 16
ITERS = 8


ridge = 0.1


def apply_operator(direction, gram, tile_panels, weights):
    dir_bf = direction.astype(jnp.bfloat16).reshape(USER_BLOCKS, BLOCK, RANK)
    scores = jnp.einsum("ubr,utir->utbi", dir_bf, tile_panels, preferred_element_type=jnp.float32)
    weighted = (weights.astype(jnp.float32) * scores).astype(jnp.bfloat16)
    back = jnp.einsum("utbi,utir->ubr", weighted, tile_panels, preferred_element_type=jnp.float32)
    back = back.reshape(USER_BLOCKS * BLOCK, RANK)
    return jnp.dot(direction, gram, precision=lax.Precision.HIGHEST) + ridge * direction + back


def solve_users(gram, tile_panels, weights):
    observed = (weights > 0).astype(jnp.float32)
    target = ((1.0 + weights.astype(jnp.float32)) * observed).astype(jnp.bfloat16)
    right_side = jnp.einsum(
        "utbi,utir->ubr", target, tile_panels, preferred_element_type=jnp.float32
    )
    right_side = right_side.reshape(USER_BLOCKS * BLOCK, RANK)
    solution = jnp.zeros_like(right_side)
    residual = right_side
    direction = right_side
    norm_now = jnp.sum(residual * residual, axis=1, keepdims=True)
    for step in range(ITERS):
        image = apply_operator(direction, gram, tile_panels, weights)
        alpha = norm_now / jnp.sum(direction * image, axis=1, keepdims=True)
        solution = solution + alpha * direction
        residual = residual - alpha * image
        norm_next = jnp.sum(residual * residual, axis=1, keepdims=True)
        direction = residual + norm_next / norm_now * direction
        norm_now = norm_next
    return solution


def shards(item_factors, send_list, route_list, tile_slot, confidence):
    partial_gram = lax.dot_general(
        item_factors, item_factors, (((0,), (0,)), ((), ())), preferred_element_type=jnp.float32
    )
    gram = lax.psum(partial_gram, ("grp", "dev"))
    own_panels = item_factors.reshape(PANELS_DEV, BLOCK, RANK)
    outgoing = own_panels[send_list[0]]
    arrived = lax.all_to_all(outgoing, "grp", split_axis=0, concat_axis=0, tiled=True)
    group_pool = arrived.reshape(-1, BLOCK, RANK)
    pool_size = group_pool.shape[0]
    everyone = lax.all_gather(group_pool, "dev", axis=0, tiled=True)
    all_routes = lax.all_gather(route_list, "dev", axis=0, tiled=True)
    member = lax.axis_index("dev")
    mine = lax.dynamic_index_in_dim(all_routes, member, 1, keepdims=False)
    sources = jnp.arange(lax.axis_size("dev"), dtype=jnp.int32)[:, None] * pool_size
    panels = everyone[(sources + mine).reshape(-1)]
    tile_panels = panels[tile_slot[0]].reshape(USER_BLOCKS, TILES_PER, BLOCK, RANK)
    weights = confidence.reshape(USER_BLOCKS, TILES_PER, BLOCK, BLOCK)
    return solve_users(gram, tile_panels, weights)


def solution(mesh):
    placed = (
        P(("grp", "dev"), None),
        P(("grp", "dev"), None, None),
        P(("grp", "dev"), None, None),
        P(("grp", "dev"), None),
        P(("grp", "dev"), None, None),
    )
    return jax.shard_map(
        shards, mesh=mesh, in_specs=placed, out_specs=P(("grp", "dev"), None), check_vma=False
    )
```

profile of v0, /device:TPU:1, one launch (start us, length us, event | category | flops | bytes accessed | tf_op | source)
XLA Modules:
  0.0 421.5 jit_solution(9784885484146711906)
XLA Ops:
  7.4 0.8 fusion.33
  8.9 15.6 %all_to_all.5 = bf16[8,1,128,256]{3,2,1,0:T(8,128)(2,1)} all-to-all(bf16[8,1,128,256]{3,2,1,0:T(8,128)(2,1)S(1)} %bitcast.238), channel_id=1, replica_groups=mesh['grp'=8,'dev'=32] {'grp'}, dimensions={0} | all-to-all | bytes 1048576 | tf_op jit(solution)/shard_map/all_to_all | solution.py:55
  24.5 0.9 fusion.45
  25.5 3.4 copy.9
  29.5 36.8 %all_gather.7 = s32[32,32,1]{1,2,0:T(1,128)S(1)} all-gather(s32[1,32,1]{1,2,0:T(1,128)S(1)} %copy-done.12), channel_id=1, replica_groups=mesh['grp'=8,'dev'=32] {'dev'}, dimensions={0}, use_global_device_ids=true | all-gather | bytes 4224 | tf_op jit(solution)/shard_map/all_gather | solution.py:59
  67.1 2.1 copy.8
  69.2 95.5 %all-gather.3.cloned.1.call-done = bf16[256,1,128,256]{3,2,1,0:T(8,128)(2,1)} async-done(((bf16[8,1,128,256]{3,2,1,0:T(8,128)(2,1)}), bf16[256,1,128,256]{3,2,1,0:T(8,128)(2,1)}) %all-gather.3.cloned.1.call-update) | async-done | bytes 16777232 | tf_op jit(solution)/shard_map/all_gather | solution.py:58
  164.7 6.5 %gather_fusion.1 = bf16[32,128,256]{2,1,0:T(8,128)(2,1)S(1)} fusion(bf16[256,128,256]{2,1,0:T(8,128)(2,1)} %bitcast.247, s32[1024]{0:T(1024)S(1)} %pad_clamp_fusion.1), kind=kCustom, calls=%fused_computation.1 | custom fusion | bytes 4194432 | tf_op jit(solution)/shard_map/gather | solution.py:63
  171.2 2.7 gather_fusion.2
  173.9 4.9 %fusion.29 = (f32[4,128]{1,0:T(4,128)S(1)}, f32[4,128,256,1]{2,1,3,0:T(8,128)S(1)}) fusion(bf16[4,16,128,256]{3,2,1,0:T(8,128)(2,1)} %bitcast.211, pred[4,16,128,128]{2,3,1,0:T(32,128)(4,1)} %bitcast.230, f32[4,16,128,128]{2,3,1,0:T(8,128)} %bitcast.220), kind=kOutput, calls=%fused_computation.52 | convolution fusion | flops 540278272 | bytes 9963520 | tf_op jit(solution)/shard_map/utbi,utir->ubr/dot_general | solution.py:29
  178.9 6.5 %fusion.11 = f32[4,128,256,1]{2,1,3,0:T(8,128)S(1)} fusion(bf16[4,16,128,256]{3,2,1,0:T(8,128)(2,1)} %bitcast.212, f32[4,16,128,128]{2,3,1,0:T(8,128)} %bitcast.221, f32[4,128,256,1]{2,1,3,0:T(8,128)S(1)} %get-tuple-element.32), kind=kOutput, calls=%fused_computation.23 | convolution fusion | flops 1075970048 | bytes 9437184 | tf_op jit(solution)/shard_map/utbi,utir->ubr/dot_general | solution.py:21
  185.4 153.0 %all-reduce.2.cloned.1.call-done = f32[256,256]{1,0:T(8,128)} async-done(((f32[256,256]{1,0:T(8,128)}), f32[256,256]{1,0:T(8,128)}) %all-reduce.2.cloned.1.call-update) | async-done | bytes 262160 | tf_op jit(solution)/shard_map/psum | solution.py:52
  338.4 1.6 multiply_reduce_fusion.13
  340.5 6.5 %fusion.12 = f32[4,128,256,1]{2,1,3,0:T(8,128)S(1)} fusion(bf16[4,16,128,256]{3,2,1,0:T(8,128)(2,1)} %bitcast.213, f32[4,16,128,128]{2,3,1,0:T(8,128)} %bitcast.222, bf16[4,128,256,1]{2,1,3,0:T(8,128)(2,1)S(1)} %bitcast.241), kind=kOutput, calls=%fused_computation.24 | convolution fusion | flops 1075838976 | bytes 9175040 | tf_op jit(solution)/shard_map/utbi,utir->ubr/dot_general | solution.py:21
  348.2 6.5 %fusion.13 = f32[4,128,256,1]{2,1,3,0:T(8,128)S(1)} fusion(bf16[4,16,128,256]{3,2,1,0:T(8,128)(2,1)} %bitcast.214, f32[4,16,128,128]{2,3,1,0:T(8,128)} %bitcast.223, bf16[4,128,256,1]{2,1,3,0:T(8,128)(2,1)S(1)} %bitcast.242), kind=kOutput, calls=%fused_computation.25 | convolution fusion | flops 1075838976 | bytes 9175040 | tf_op jit(solution)/shard_map/utbi,utir->ubr/dot_general | solution.py:21
  355.6 0.8 fusion.42
  356.4 6.8 %fusion.14 = f32[4,128,256,1]{2,1,3,0:T(8,128)S(1)} fusion(bf16[4,16,128,256]{3,2,1,0:T(8,128)(2,1)} %bitcast.215, f32[4,16,128,128]{2,3,1,0:T(8,128)} %bitcast.224, bf16[4,128,256,1]{2,1,3,0:T(8,128)(2,1)} %bitcast.243), kind=kOutput, calls=%fused_computation.26 | convolution fusion | flops 1075838976 | bytes 9175040 | tf_op jit(solution)/shard_map/utbi,utir->ubr/dot_general | solution.py:21
  364.5 0.8 fusion.41
  365.3 7.3 %fusion.15 = f32[4,128,256,1]{2,1,3,0:T(8,128)} fusion(bf16[4,16,128,256]{3,2,1,0:T(8,128)(2,1)} %bitcast.216, f32[4,16,128,128]{2,3,1,0:T(8,128)} %bitcast.225, bf16[4,128,256,1]{2,1,3,0:T(8,128)(2,1)} %bitcast.244), kind=kOutput, calls=%fused_computation.27 | convolution fusion | flops 1075838976 | bytes 9175040 | tf_op jit(solution)/shard_map/utbi,utir->ubr/dot_general | solution.py:21
  372.6 1.7 multiply_reduce_fusion.5
  374.6 0.8 copy-done.5
  375.4 0.8 fusion.40
  376.3 7.5 %fusion.16 = f32[4,128,256,1]{2,1,3,0:T(8,128)} fusion(bf16[4,16,128,256]{3,2,1,0:T(8,128)(2,1)} %bitcast.217, f32[4,16,128,128]{2,3,1,0:T(8,128)} %bitcast.226, bf16[4,128,256,1]{2,1,3,0:T(8,128)(2,1)} %bitcast.245), kind=kOutput, calls=%fused_computation.28 | convolution fusion | flops 1075838976 | bytes 9175040 | tf_op jit(solution)/shard_map/utbi,utir->ubr/dot_general | solution.py:21
  383.8 1.7 multiply_reduce_fusion.3
  385.5 1.3 multiply_reduce_fusion.2
  386.8 2.1 fusion.39
  388.9 7.4 %fusion.17 = f32[4,128,256,1]{2,1,3,0:T(8,128)} fusion(bf16[4,16,128,256]{3,2,1,0:T(8,128)(2,1)} %bitcast.218, f32[4,16,128,128]{2,3,1,0:T(8,128)} %bitcast.227, bf16[4,128,256,1]{2,1,3,0:T(8,128)(2,1)} %bitcast.246), kind=kOutput, calls=%fused_computation.29 | convolution fusion | flops 1075838976 | bytes 9175040 | tf_op jit(solution)/shard_map/utbi,utir->ubr/dot_general | solution.py:21
  396.3 2.1 multiply_reduce_fusion.1
  399.2 2.2 fusion.38
  401.3 7.4 %fusion.18 = f32[4,128,256,1]{2,1,3,0:T(8,128)} fusion(bf16[4,16,128,256]{3,2,1,0:T(8,128)(2,1)} %bitcast.219, f32[4,16,128,128]{2,3,1,0:T(8,128)} %bitcast.228, bf16[4,128,256,1]{2,1,3,0:T(8,128)(2,1)} %bitcast.240), kind=kOutput, calls=%fused_computation.30 | convolution fusion | flops 1075838976 | bytes 9175040 | tf_op jit(solution)/shard_map/utbi,utir->ubr/dot_general | solution.py:21
  408.8 2.0 fusion.28
  411.5 2.6 multiply_add_fusion
  (65 shorter events, 7.7 us)
Async XLA Ops:
  7.4 0.9 copy-start
  7.4 18.1 %copy-start.2 = (bf16[64,128,128]{2,1,0:T(8,128)(2,1)S(1)}, bf16[64,128,128]{2,1,0:T(8,128)(2,1)}, u32[]{:S(2)}) copy-start(bf16[64,128,128]{2,1,0:T(8,128)(2,1)} %param.9) | copy-start | bytes 6291460
  7.4 157.3 %all-gather.3.cloned.1.call-start = ((), (), s32[]{:S(2)}) async-start(), calls=%async_computation.2 | async-start | bytes 17301504 | tf_op jit(solution)/shard_map/all_gather | solution.py:58
  24.5 313.9 %all-reduce.2.cloned.1.call-start = ((), (), s32[]{:S(2)}) async-start(), calls=%async_computation.1 | async-start | bytes 524288 | tf_op jit(solution)/shard_map/psum | solution.py:52
  25.5 4.0 copy-start.12
  25.5 41.5 %copy-start.13 = (s32[1,64]{1,0:T(1,128)S(1)}, s32[1,64]{1,0:T(1,128)}, u32[]{:S(2)}) copy-start(s32[1,64]{1,0:T(1,128)} %param.8) | copy-start | bytes 772
  340.5 6.5 %copy-start.1 = (f32[256,256]{1,0:T(8,128)S(1)}, f32[256,256]{1,0:T(8,128)}, u32[]{:S(2)}) copy-start(f32[256,256]{1,0:T(8,128)} %all-reduce.2.cloned.1.call-done) | copy-start | bytes 786436
  355.3 7.9 %copy-start.6 = (f32[512]{0:T(512)}, f32[512]{0:T(512)S(1)}, u32[]{:S(2)}) copy-start(f32[512]{0:T(512)S(1)} %div.124) | copy-start | bytes 6148
  363.9 0.6 copy-start.8
  374.4 1.9 copy-start.9
  374.6 0.8 copy-start.5
  376.3 7.5 %copy-start.3 = (f32[512,256]{1,0:T(8,128)}, f32[512,256]{1,0:T(8,128)S(1)}, u32[]{:S(2)}) copy-start(f32[512,256]{1,0:T(8,128)S(1)} %get-tuple-element.12) | copy-start | bytes 1572868
  385.5 1.3 copy-start.10
  398.6 0.6 copy-start.11
  401.3 10.1 %copy-start.4 = (f32[512,256]{1,0:T(8,128)S(1)}, f32[512,256]{1,0:T(8,128)}, u32[]{:S(2)}) copy-start(f32[512,256]{1,0:T(8,128)} %copy-done.3) | copy-start | bytes 1572868
  401.3 10.1 %copy-start.7 = (f32[512]{0:T(512)S(1)}, f32[512]{0:T(512)}, u32[]{:S(2)}) copy-start(f32[512]{0:T(512)} %copy-done.6) | copy-start | bytes 6148
Sparse Core Ops, SparseCore 0:
  24.6 140.0 all-gather.2
Sparse Core Ops, SparseCore 1:
  30.4 307.9 all-reduce.1
where the time goes:
time: 423 us; the launch traced here: 421 us
  waiting for transfers between devices  249 us (59%)
  matrix products  72.9 us (17%)
  blocking collectives  52.4 us (12%)
  local copies, waits for them, and re-layouts  17.8 us (4%)
  between operations  15.1 us (4%)
  other arithmetic  14.6 us (3%)
    psum x1, waiting for transfers between devices, shards(): gram = lax.psum(partial_gram, ('grp', 'dev'))  153 us
    all_gather x1, waiting for transfers between devices, shards(): everyone = lax.all_gather(group_pool, 'dev', axis=0, tiled=True)  95.5 us
    dot_general x8, matrix products, apply_operator(): jnp.einsum('utbi,utir->ubr', weighted, tile_panels, preferred_element_typ...  55.9 us
    all_gather x1, blocking collectives, shards(): all_routes = lax.all_gather(route_list, 'dev', axis=0, tiled=True)  36.8 us
    all_to_all x1, blocking collectives, shards(): lax.all_to_all(outgoing, 'grp', split_axis=0, concat_axis=0, tiled=True)  15.6 us
    dot_general x8, matrix products, apply_operator(): jnp.dot(direction, gram, precision=lax.Precision.HIGHEST)  11.2 us
  transfers between devices with their start and end apart: 2, of which 2 were waited for; matrix products, arithmetic and copies ran while one was open for 7% of the time, Pallas kernels for 0%

commit v1 on v0

v1 whole, which is shorter than its diff:
```python
import functools

import jax
import jax.numpy as jnp
from jax import lax
from jax.experimental import pallas as pl
from jax.experimental.pallas import tpu as pltpu
from jax.sharding import PartitionSpec as P

PANELS_DEV=2; RANK=256; BLOCK=128; UB=4; TP=16; ITERS=8; RIDGE=0.1
F32=jnp.float32; BF=jnp.bfloat16
NT=(((1,),(1,)),((),()))
def dot(a,b): return jnp.dot(a,b,preferred_element_type=F32)

def cg_kernel(CH, PT, slot_ref, gram_ref, conf_ref, slots_ref, out_ref, pan, pant, gh, gl, res, dirn, rr):
    W=UB*TP
    def gather(t,_):
        p=slots_ref[slot_ref[0,t]]
        pan[pl.ds(pl.multiple_of(t*BLOCK,BLOCK),BLOCK),:]=p
        return 0
    lax.fori_loop(0,W,gather,0,unroll=4)
    if PT:
        def tr(q,_):
            p=pan[pl.ds(pl.multiple_of(q*256,256),256),:]
            pant[pl.ds(pl.multiple_of(q*256,256),256),:]=p.T
            return 0
        lax.fori_loop(0,W//2,tr,0)
    g=gram_ref[...]
    h=g.astype(BF); gh[...]=h; gl[...]=(g-h.astype(F32)).astype(BF)
    NC=TP*BLOCK//CH; TC=CH//BLOCK
    def tiles(b,c): return [b*TP+c*TC+j for j in range(TC)]
    def rows(b,c): return slice((b*TP+c*TC)*BLOCK,(b*TP+c*TC+TC)*BLOCK)
    for b in range(UB):
        acc=None
        for c in range(NC):
            w=jnp.concatenate([conf_ref[t] for t in tiles(b,c)],axis=1).astype(F32)
            tgt=jnp.where(w>0,1.0+w,0.0).astype(BF)
            d=dot(tgt,pan[rows(b,c),:])
            acc=d if acc is None else acc+d
        us=slice(b*BLOCK,(b+1)*BLOCK)
        res[us,:]=acc; dirn[us,:]=acc
        out_ref[us,:]=jnp.zeros_like(acc)
        rr[us,:]=jnp.broadcast_to(jnp.sum(acc*acc,axis=1,keepdims=True),(BLOCK,128))
    def it(i,_):
        for b in range(UB):
            us=slice(b*BLOCK,(b+1)*BLOCK)
            v=dirn[us,:]
            vb=v.astype(BF); vl=(v-vb.astype(F32)).astype(BF)
            acc=dot(vb,gh[...])+dot(vb,gl[...])+dot(vl,gh[...])+RIDGE*v
            for c in range(NC):
                if PT:
                    s=jnp.concatenate([dot(vb,pant[(b*TP+c*TC+2*j)*BLOCK:(b*TP+c*TC+2*j+2)*BLOCK,:]) for j in range(TC//2)],axis=1)
                else:
                    s=lax.dot_general(vb,pan[rows(b,c),:],NT,preferred_element_type=F32)
                w=jnp.concatenate([conf_ref[t] for t in tiles(b,c)],axis=1).astype(F32)
                ws=(w*s).astype(BF)
                acc=acc+dot(ws,pan[rows(b,c),:])
            r0=rr[us,0:1]
            alpha=r0/jnp.sum(v*acc,axis=1,keepdims=True)
            out_ref[us,:]=out_ref[us,:]+alpha*v
            r=res[us,:]-alpha*acc
            r1=jnp.sum(r*r,axis=1,keepdims=True)
            res[us,:]=r
            dirn[us,:]=r+(r1/r0)*v
            rr[us,:]=jnp.broadcast_to(r1,(BLOCK,128))
        return 0
    lax.fori_loop(0,ITERS,it,0)

def cg(slot, gram, conf, slots, CH=512, PT=False):
    vm=pl.BlockSpec(memory_space=pltpu.VMEM)
    return pl.pallas_call(functools.partial(cg_kernel,CH,PT),
        out_shape=jax.ShapeDtypeStruct((UB*BLOCK,RANK),F32),
        in_specs=[pl.BlockSpec(memory_space=pltpu.SMEM),vm,vm,vm], out_specs=vm,
        scratch_shapes=[pltpu.VMEM((UB*TP*BLOCK,RANK),BF),pltpu.VMEM((UB*TP*BLOCK,RANK),BF),
          pltpu.VMEM((RANK,RANK),BF),pltpu.VMEM((RANK,RANK),BF),
          pltpu.VMEM((UB*BLOCK,RANK),F32),pltpu.VMEM((UB*BLOCK,RANK),F32),pltpu.VMEM((UB*BLOCK,128),F32)],
        name="cg", compiler_params=pltpu.CompilerParams(vmem_limit_bytes=48<<20))(slot,gram,conf,slots)


MESH = pl.DeviceIdType.MESH
NG, NX, NZ = 8, 4, 8
ND = NX * NZ
HALF1 = ((4, 0), (3, 0), (5, 0), (2, 0), (6, 0))


def comm_kernel(order, split, send_ref, route_ref, items_ref, slots_ref, gram_ref,
                pool, out1, out2, part, g1, g2, g3, s2, s3, s4,
                ss1, rs1, ss2, rs2, gs1, gr1, gs2, gr2, gs3, gr3, gs4, gr4, gs5, gr5):
    g = lax.axis_index("grp")
    d = lax.axis_index("dev")
    z, x = d // NX, lax.rem(d, NX)
    grp_peers = [lax.rem(g + k, NG) for k in range(1, NG)]
    x_peers = [lax.rem(x + k, NX) for k in range(1, NX)]
    z_peers = [lax.rem(z + k, NZ) for k in range(1, NZ)]

    barrier = pltpu.get_barrier_semaphore()
    for p in grp_peers:
        pl.semaphore_signal(barrier, inc=1, device_id={"grp": p}, device_id_type=MESH)
    for k in range(1, ND):
        pl.semaphore_signal(barrier, inc=1, device_id={"dev": lax.rem(d + k, ND)}, device_id_type=MESH)

    def send(src, dst, ss, rs, where):
        c = pltpu.make_async_remote_copy(
            src_ref=src, dst_ref=dst, send_sem=ss, recv_sem=rs, device_id=where, device_id_type=MESH)
        c.start()
        return c

    def arrived(ref, ss, rs, where):
        pltpu.make_async_remote_copy(
            src_ref=ref, dst_ref=ref, send_sem=ss, recv_sem=rs, device_id=where, device_id_type=MESH).wait_recv()

    flat = items_ref[...].reshape(PANELS_DEV * BLOCK, RANK)
    part[...] = lax.dot_general(flat, flat, (((0,), (0,)), ((), ())), preferred_element_type=F32)
    for j in range(NG):
        out1[j] = items_ref[send_ref[0, j, 0]]
    pool[g] = out1[g]
    g1[g] = part[pl.ds(pl.multiple_of(g * 32, 32), 32), :]
    pl.semaphore_wait(barrier, NG - 1 + ND - 1)

    sent = []
    for p in grp_peers:
        sent.append(send(part.at[pl.ds(pl.multiple_of(p * 32, 32), 32), :], g1.at[g], gs1.at[p], gr1.at[g], {"grp": p}))
    for p in grp_peers:
        sent.append(send(out1.at[p], pool.at[g], ss1.at[p], rs1.at[g], {"grp": p}))
    for p in grp_peers:
        arrived(g1.at[p], gs1.at[p], gr1.at[p], {"grp": p})
    total = g1[0]
    for j in range(1, NG):
        total = total + g1[j]
    s2[...] = total.reshape(NX, 8, RANK)
    g2[x] = s2[x]
    for p in x_peers:
        sent.append(send(s2.at[p], g2.at[x], gs2.at[p], gr2.at[x], {"dev": z * NX + p}))
    for p in x_peers:
        arrived(g2.at[p], gs2.at[p], gr2.at[p], {"dev": z * NX + p})
    s3[...] = (g2[0] + g2[1]) + (g2[2] + g2[3])
    g3[z] = s3[...]
    for p in z_peers:
        sent.append(send(s3, g3.at[z], gs3.at[p], gr3.at[z], {"dev": p * NX + x}))

    for p in grp_peers:
        arrived(pool.at[p], ss1.at[p], rs1.at[p], {"grp": p})

    dests = [(lax.rem(z + dz, NZ) * NX + lax.rem(x + dx, NX)) for dz, dx in order]

    def fill(e):
        out2[e] = pool[route_ref[0, e, 0]]

    def ship(e):
        sent.append(send(out2.at[e], slots_ref.at[d], ss2.at[e], rs2.at[d], {"dev": e}))

    fill(dests[0])
    fill(dests[1])
    for i in range(len(dests)):
        if i + 2 < len(dests):
            fill(dests[i + 2])
        ship(dests[i])
        if i == split:
            for p in z_peers:
                arrived(g3.at[p], gs3.at[p], gr3.at[p], {"dev": p * NX + x})
            tot = g3[0]
            for j in range(1, NZ):
                tot = tot + g3[j]
            s4[x] = tot
            for p in x_peers:
                sent.append(send(s4.at[x], s4.at[x], gs4.at[p], gr4.at[x], {"dev": z * NX + p}))
    slots_ref[d] = pool[route_ref[0, d, 0]]
    for p in x_peers:
        arrived(s4.at[p], gs4.at[p], gr4.at[p], {"dev": z * NX + p})
    gram_ref[g] = s4[...]
    for p in grp_peers:
        sent.append(send(s4, gram_ref.at[g], gs5.at[p], gr5.at[g], {"grp": p}))
    for p in grp_peers:
        arrived(gram_ref.at[p], gs5.at[p], gr5.at[p], {"grp": p})
    for e in dests:
        arrived(slots_ref.at[e], ss2.at[e], rs2.at[e], {"dev": e})
    for c in sent:
        c.wait_send()


ORDER = tuple((dz, dx) for dz in (4, 3, 5, 2, 6, 1, 7, 0) for dx in range(NX) if (dz, dx) != (0, 0))


def comm(send_list, route_list, items, order=ORDER, split=15):
    vm = pl.BlockSpec(memory_space=pltpu.VMEM)
    sm = pl.BlockSpec(memory_space=pltpu.SMEM)
    dma = pltpu.SemaphoreType.DMA
    slots, gram = pl.pallas_call(
        functools.partial(comm_kernel, order, split),
        out_shape=(jax.ShapeDtypeStruct((ND, BLOCK, RANK), BF), jax.ShapeDtypeStruct((NG, NX, 8, RANK), F32)),
        in_specs=[sm, sm, vm],
        out_specs=(vm, vm),
        scratch_shapes=[
            pltpu.VMEM((NG, BLOCK, RANK), BF),
            pltpu.VMEM((NG, BLOCK, RANK), BF),
            pltpu.VMEM((ND, BLOCK, RANK), BF),
            pltpu.VMEM((RANK, RANK), F32),
            pltpu.VMEM((NG, 32, RANK), F32),
            pltpu.VMEM((NX, 8, RANK), F32),
            pltpu.VMEM((NZ, 8, RANK), F32),
            pltpu.VMEM((NX, 8, RANK), F32),
            pltpu.VMEM((8, RANK), F32),
            pltpu.VMEM((NX, 8, RANK), F32),
            dma((NG,)), dma((NG,)), dma((ND,)), dma((ND,)),
            dma((NG,)), dma((NG,)), dma((NX,)), dma((NX,)), dma((NZ,)), dma((NZ,)),
            dma((NX,)), dma((NX,)), dma((NG,)), dma((NG,)),
        ],
        name="exchange",
        compiler_params=pltpu.CompilerParams(collective_id=0, has_side_effects=True, vmem_limit_bytes=32 << 20),
    )(send_list, route_list, items)
    return slots, gram.reshape(RANK, RANK)


def shards(item_factors, send_list, route_list, tile_slot, confidence):
    own_panels = item_factors.reshape(-1, BLOCK, RANK)
    slots, gram = comm(send_list, route_list, own_panels)
    return cg(tile_slot, gram, confidence, slots, CH=1024, PT=True)


def solution(mesh):
    placed = (
        P(("grp", "dev"), None),
        P(("grp", "dev"), None, None),
        P(("grp", "dev"), None, None),
        P(("grp", "dev"), None),
        P(("grp", "dev"), None, None),
    )
    return jax.shard_map(
        shards, mesh=mesh, in_specs=placed, out_specs=P(("grp", "dev"), None), check_vma=False
    )
```

time: 423 us -> 101 us (0.24)
  waiting for transfers between devices: 249 us -> 0 us
  Pallas kernels: 0 us -> 96.3 us
  matrix products: 72.9 us -> 0 us
  blocking collectives: 52.4 us -> 0 us
  between operations: 15.1 us -> 0.02 us
  other arithmetic: 14.6 us -> 0 us
  local copies, waits for them, and re-layouts: 17.8 us -> 4.61 us
    psum x1 -> x0, waiting for transfers between devices: 153 us -> none  [shards(): gram = lax.psum(partial_gram, ('grp', 'dev'))]
    pallas_call x0 -> x2, Pallas kernels: none -> 96.3 us  [the longest x1 74.2 us: comm(): pl.pallas_call(functools.partial(comm_kernel, order, split), out_shape=(j...]
    all_gather x1 -> x0, waiting for transfers between devices: 95.5 us -> none  [shards(): everyone = lax.all_gather(group_pool, 'dev', axis=0, tiled=True)]
    dot_general x18 -> x0, matrix products: 72.9 us -> none  [the longest x8 55.9 us: apply_operator(): jnp.einsum('utbi,utir->ubr', weighted, tile_panels, preferred_element_typ...]
    all_gather x1 -> x0, blocking collectives: 36.8 us -> none  [shards(): all_routes = lax.all_gather(route_list, 'dev', axis=0, tiled=True)]
    all_to_all x1 -> x0, blocking collectives: 15.6 us -> none  [shards(): lax.all_to_all(outgoing, 'grp', split_axis=0, concat_axis=0, tiled=True)]
    gather x3 -> x0, local copies, waits for them, and re-layouts: 9.8 us -> none  [the longest x1 6.48 us: shards(): panels = everyone[(sources + mine).reshape(-1)]]
    convert_element_type x7 -> x0, other arithmetic: 7.09 us -> none  [apply_operator(): dir_bf = direction.astype(jnp.bfloat16).reshape(USER_BLOCKS, BLOCK, RANK)]
  transfers between devices with their start and end apart: 2 -> 0, of which waited for: 2 -> 0; matrix products, arithmetic and copies ran while one was open for 7% -> 0% of each run, Pallas kernels for 0% -> 0%
where the time goes in v1:
time: 101 us
  Pallas kernels  96.3 us (95%)
  local copies, waits for them, and re-layouts  4.61 us (5%)
    pallas_call x1, Pallas kernels, comm(): pl.pallas_call(functools.partial(comm_kernel, order, split), out_shape=(j...  74.2 us
    pallas_call x1, Pallas kernels, cg(): pl.pallas_call(functools.partial(cg_kernel, CH, PT), out_shape=jax.ShapeD...  22.1 us
    unnamed x8, local copies, waits for them, and re-layouts  4.61 us

profile of v1, /device:TPU:1, one launch (start us, length us, event | category | flops | bytes accessed | tf_op | source)
XLA Modules:
  0.0 100.9 jit_solution(12462437086919427074)
XLA Ops:
  0.0 0.7 copy.6.send_ref
  0.7 0.7 copy.7.route_ref
  1.5 0.0 copy-start.1
  1.5 0.9 copy-done.1
  2.4 74.2 %exchange.1 = (bf16[32,128,256]{2,1,0:T(8,128)(2,1)S(1)}, f32[8,4,8,256]{3,2,1,0:T(8,128)S(1)}) custom-call(s32[1,8,1]{2,1,0:T(8,128)S(1)} %copy.6.send_ref, s32[1,32,1]{2,1,0:T(8,128)S(1)} %copy.7.route_ref, bf16[2,128,256]{2,1,0:T(8,128)(2,1)S(1)} %bitcast.3), custom_call_target="tpu_custom_call" | custom-call | tf_op jit(solution)/shard_map/exchange/pallas_call | solution.py:188
  76.5 0.0 copy-start
  76.6 1.6 %copy-done = bf16[64,128,128]{2,1,0:T(8,128)(2,1)S(1)} copy-done((bf16[64,128,128]{2,1,0:T(8,128)(2,1)S(1)}, bf16[64,128,128]{2,1,0:T(8,128)(2,1)}, u32[]{:S(2)}) %copy-start) | copy-done | bytes 2097176
  78.1 0.0 copy-start.2
  78.1 0.7 copy-done.2
  78.8 22.1 %cg.1 = f32[512,256]{1,0:T(8,128)} custom-call(s32[1,64]{1,0:T(1,128)S(1)} %copy-done.2, f32[256,256]{1,0:T(8,128)S(1)} %bitcast.2, bf16[64,128,128]{2,1,0:T(8,128)(2,1)S(1)} %copy-done, bf16[32,128,256]{2,1,0:T(8,128)(2,1)S(1)} %get-tuple-element.8.slots_ref), custom_call_target="tpu_custom_call" | custom-call | tf_op jit(solution)/shard_map/cg/pallas_call | solution.py:71
Async XLA Ops:
  1.5 0.9 copy-start.1
  76.5 1.6 %copy-start = (bf16[64,128,128]{2,1,0:T(8,128)(2,1)S(1)}, bf16[64,128,128]{2,1,0:T(8,128)(2,1)}, u32[]{:S(2)}) copy-start(bf16[64,128,128]{2,1,0:T(8,128)(2,1)} %conf_ref.1) | copy-start | bytes 6291460
  78.1 0.7 copy-start.2

commit v2 on v0

v2 whole, which is shorter than its diff:
```python
import functools

import jax
import jax.numpy as jnp
from jax import lax
from jax.experimental import pallas as pl
from jax.experimental.pallas import tpu as pltpu
from jax.sharding import PartitionSpec as P

PANELS_DEV = 2
RANK = 256
BLOCK = 128
UB = 4
TP = 16
ITERS = 8
RIDGE = 0.1
NG, NY, NC, NX, NZ = 8, 4, 2, 4, 8
ND = NX * NZ
SEND_AT, ROUTE_AT, SLOT_AT = 0, 8, 40
F32 = jnp.float32
BF = jnp.bfloat16
MESH = pl.DeviceIdType.MESH
FAR = (3, 5, 4)
NEAR = tuple((dz, dx) for dz in (2, 6, 1, 7, 0) for dx in (2, 1, 3, 0) if (dz, dx) != (0, 0))
FIRST = 10
CHUNK = 1024


def dot(a, b):
    return jnp.dot(a, b, preferred_element_type=F32)


def half(ref, i):
    return ref.at[pl.ds(pl.multiple_of(i * 128, 128), 128), :]


def solve(meta, slots, gram, conf, out, pan, pant, gh, gl, res, dirn, rr):
    tiles = UB * TP

    def gather(t, carry):
        pan[pl.ds(pl.multiple_of(t * BLOCK, BLOCK), BLOCK), :] = slots[meta[0, SLOT_AT + t]]
        return carry

    lax.fori_loop(0, tiles, gather, 0, unroll=4)

    def turn(q, carry):
        rows = pl.ds(pl.multiple_of(q * 256, 256), 256)
        pant[rows, :] = pan[rows, :].T
        return carry

    lax.fori_loop(0, tiles // 2, turn, 0)
    g = gram[...].reshape(RANK, RANK)
    high = g.astype(BF)
    gh[...] = high
    gl[...] = (g - high.astype(F32)).astype(BF)
    per = CHUNK // BLOCK
    chunks = TP // per

    def confs(b, c):
        return jnp.concatenate([conf[b * TP + c * per + j] for j in range(per)], axis=1).astype(F32)

    def rows(b, c):
        return slice((b * TP + c * per) * BLOCK, (b * TP + c * per + per) * BLOCK)

    for b in range(UB):
        acc = None
        for c in range(chunks):
            w = confs(b, c)
            d = dot(jnp.where(w > 0, 1.0 + w, 0.0).astype(BF), pan[rows(b, c), :])
            acc = d if acc is None else acc + d
        us = slice(b * BLOCK, (b + 1) * BLOCK)
        res[us, :] = acc
        dirn[us, :] = acc
        out[us, :] = jnp.zeros_like(acc)
        rr[us, :] = jnp.broadcast_to(jnp.sum(acc * acc, axis=1, keepdims=True), (BLOCK, 128))

    def step(i, carry):
        for b in range(UB):
            us = slice(b * BLOCK, (b + 1) * BLOCK)
            v = dirn[us, :]
            vb = v.astype(BF)
            vl = (v - vb.astype(F32)).astype(BF)
            acc = dot(vb, gh[...]) + dot(vb, gl[...]) + dot(vl, gh[...]) + RIDGE * v
            for c in range(chunks):
                first = (b * TP + c * per) * BLOCK
                s = jnp.concatenate(
                    [dot(vb, pant[first + 256 * j : first + 256 * j + 256, :]) for j in range(per // 2)], axis=1
                )
                acc = acc + dot((confs(b, c) * s).astype(BF), pan[rows(b, c), :])
            old = rr[us, 0:1]
            alpha = old / jnp.sum(v * acc, axis=1, keepdims=True)
            out[us, :] = out[us, :] + alpha * v
            r = res[us, :] - alpha * acc
            new = jnp.sum(r * r, axis=1, keepdims=True)
            res[us, :] = r
            dirn[us, :] = r + (new / old) * v
            rr[us, :] = jnp.broadcast_to(new, (BLOCK, 128))
        return carry

    lax.fori_loop(0, ITERS, step, 0)


def exchange(meta_v, meta, items, slots, gram, raw, metas_v, metas, pools, out1, out2, out3, part,
             gc, sc, gy, s2, g2, s3, g3, s4, local, sm, rm, sr, rr, sp, rp, sn, rs, sx,
             cs, cr, ys, yr, xs, xr, zs, zr, as_, ar, bs, br, es, er, before_wait):
    g = lax.axis_index("grp")
    d = lax.axis_index("dev")
    z, x = d // NX, lax.rem(d, NX)
    y, c = g // NC, lax.rem(g, NC)
    grp_peers = [lax.rem(g + k, NG) for k in (1, 3, 5, 7, 2, 6, 4)]
    x_peers = [lax.rem(x + k, NX) for k in range(1, NX)]
    y_peers = [lax.rem(y + k, NY) for k in range(1, NY)]
    z_peers = [lax.rem(z + k, NZ) for k in range(1, NZ)]

    def at_z(k):
        return {"dev": lax.rem(z + k, NZ) * NX + x}

    def at_x(p):
        return {"dev": z * NX + p}

    def at_y(p):
        return {"grp": p * NC + c}

    other = {"grp": y * NC + 1 - c}

    barrier = pltpu.get_barrier_semaphore()
    near = [lax.rem(z + dz, NZ) * NX + lax.rem(x + dx, NX) for dz, dx in NEAR]
    for p in grp_peers:
        pl.semaphore_signal(barrier, inc=1, device_id={"grp": p}, device_id_type=MESH)
    for e in near:
        pl.semaphore_signal(barrier, inc=1, device_id={"dev": e}, device_id_type=MESH)
    for o in FAR:
        pl.semaphore_signal(barrier, inc=1, device_id=at_z(o), device_id_type=MESH)

    started = []

    def send(src, dst, ss, rs_, where):
        copy = pltpu.make_async_remote_copy(
            src_ref=src, dst_ref=dst, send_sem=ss, recv_sem=rs_, device_id=where, device_id_type=MESH
        )
        copy.start()
        started.append(copy)

    def arrived(ref, ss, rs_):
        pltpu.make_async_remote_copy(
            src_ref=ref, dst_ref=ref, send_sem=ss, recv_sem=rs_, device_id=other, device_id_type=MESH
        ).wait_recv()

    before_wait()
    flat = items[...].reshape(PANELS_DEV * BLOCK, RANK)
    part[...] = lax.dot_general(flat, flat, (((0,), (0,)), ((), ())), preferred_element_type=F32)
    for j in range(NG):
        out1[3, j] = items[meta[0, SEND_AT + j]]
    pools[3][g] = out1[3, g]
    pl.semaphore_wait(barrier, len(grp_peers) + len(near) + len(FAR))

    for i, o in enumerate(FAR):
        send(meta_v, metas_v.at[i], sm.at[i], rm.at[i], at_z(NZ - o))
    for i in range(2):
        send(items, raw[i], sr.at[i], rr.at[i], at_z(NZ - FAR[i]))
    for p in grp_peers:
        send(out1.at[3, p], pools[3].at[g], sp.at[3, p], rp.at[3, g], {"grp": p})
    send(half(part, 1 - c), gc, cs.at[0], cr.at[0], other)
    arrived(gc, cs.at[0], cr.at[0])
    sc[...] = (half(part, c)[...] + gc[...]).reshape(NY, 32, RANK)
    gy[y] = sc[y]
    for p in y_peers:
        send(sc.at[p], gy.at[y], ys.at[p], yr.at[y], at_y(p))

    def pool_ready(i):
        for p in grp_peers:
            arrived(pools[i].at[p], sp.at[i, p], rp.at[i, p])

    def fill(n):
        if n < len(near):
            out2[n] = pools[3][meta[0, ROUTE_AT + near[n]]]

    def ship(n):
        send(out2.at[n], slots.at[d], sn.at[n], rs.at[d], {"dev": near[n]})

    pool_ready(3)
    fill(0)
    fill(1)
    for n in range(FIRST):
        fill(n + 2)
        ship(n)
    for p in y_peers:
        arrived(gy.at[p], ys.at[p], yr.at[p])
    s2[...] = ((gy[0] + gy[1]) + (gy[2] + gy[3])).reshape(NX, 8, RANK)
    g2[x] = s2[x]
    for p in x_peers:
        send(s2.at[p], g2.at[x], xs.at[p], xr.at[x], at_x(p))

    def proxy(i):
        for j in range(NG):
            out1[i, j] = raw[i][metas[i, 0, SEND_AT + j]]
        pools[i][g] = out1[i, g]
        for p in grp_peers:
            send(out1.at[i, p], pools[i].at[g], sp.at[i, p], rp.at[i, g], {"grp": p})

    for i in range(3):
        arrived(metas_v.at[i], sm.at[i], rm.at[i])
        pltpu.make_async_copy(metas_v.at[i], metas.at[i], local.at[i]).start()
    for i in range(3):
        pltpu.make_async_copy(metas_v.at[i], metas.at[i], local.at[i]).wait()
    arrived(raw[0], sr.at[0], rr.at[0])
    send(raw[0].at[1], raw[2].at[1], sr.at[3], rr.at[3], at_z(NZ - 1))
    arrived(raw[1], sr.at[1], rr.at[1])
    send(raw[1].at[0], raw[2].at[0], sr.at[2], rr.at[2], at_z(1))
    proxy(0)
    proxy(1)

    for p in x_peers:
        arrived(g2.at[p], xs.at[p], xr.at[p])
    s3[...] = (g2[0] + g2[1]) + (g2[2] + g2[3])
    g3[z] = s3[...]
    for k, p in enumerate(z_peers):
        send(s3, g3.at[z], zs.at[p], zr.at[z], at_z(k + 1))

    for n in range(FIRST, len(near)):
        fill(n + 2)
        ship(n)

    arrived(raw[2].at[0], sr.at[2], rr.at[2])
    arrived(raw[2].at[1], sr.at[3], rr.at[3])
    proxy(2)

    for p in z_peers:
        arrived(g3.at[p], zs.at[p], zr.at[p])
    total = ((g3[0] + g3[1]) + (g3[2] + g3[3])) + ((g3[4] + g3[5]) + (g3[6] + g3[7]))
    s4[x] = total
    for p in x_peers:
        send(s4.at[x], s4.at[x], as_.at[p], ar.at[x], at_x(p))

    def relay(i):
        slot = lax.rem(z + FAR[i], NZ) * NX + x
        pool_ready(i)
        for k, p in enumerate(x_peers):
            out3[i, k] = pools[i][metas[i, 0, ROUTE_AT + z * NX + p]]
        for k, p in enumerate(x_peers):
            send(out3.at[i, k], slots.at[slot], sx.at[i, k], rs.at[slot], at_x(p))
        slots[slot] = pools[i][metas[i, 0, ROUTE_AT + d]]

    slots[d] = pools[3][meta[0, ROUTE_AT + d]]
    relay(0)
    relay(1)
    for p in x_peers:
        arrived(s4.at[p], as_.at[p], ar.at[p])
    gram[c, y] = s4[...]
    for p in y_peers:
        send(s4, gram.at[c, y], bs.at[p], br.at[y], at_y(p))
    relay(2)
    for p in y_peers:
        arrived(gram.at[c, p], bs.at[p], br.at[p])
    send(gram.at[c], gram.at[c], es.at[0], er.at[0], other)

    for n, e in enumerate(near):
        arrived(slots.at[e], sn.at[n], rs.at[e])
    for i, o in enumerate(FAR):
        for k, p in enumerate(x_peers):
            slot = lax.rem(z + o, NZ) * NX + p
            arrived(slots.at[slot], sx.at[i, k], rs.at[slot])
    arrived(gram.at[1 - c], es.at[0], er.at[0])
    for copy in started:
        copy.wait_send()


def kernel(meta_h, items_h, conf_h, out, meta_v, meta, items, conf, slots, gram, raw0, raw1, raw2, metas_v, metas,
           pool0, pool1, pool2, pool3, out1, out2, out3, part, gc, sc, gy, s2, g2, s3, g3, s4, pan, pant, gh, gl, res, dirn, rr, *sems):
    ins, sems = sems[0], sems[1:]
    loads = [
        pltpu.make_async_copy(meta_h, meta, ins.at[0]),
        pltpu.make_async_copy(meta_h, meta_v, ins.at[1]),
        pltpu.make_async_copy(items_h, items, ins.at[2]),
        pltpu.make_async_copy(conf_h, conf, ins.at[3]),
    ]
    for copy in loads:
        copy.start()

    def ready():
        for copy in loads[:3]:
            copy.wait()

    exchange(meta_v, meta, items, slots, gram, (raw0, raw1, raw2), metas_v, metas,
             (pool0, pool1, pool2, pool3), out1, out2, out3, part,
             gc, sc, gy, s2, g2, s3, g3, s4, *sems, ready)
    loads[3].wait()
    solve(meta, slots, gram, conf, out, pan, pant, gh, gl, res, dirn, rr)


def half_sweep(meta, items, conf):
    dma = pltpu.SemaphoreType.DMA
    hbm = pl.BlockSpec(memory_space=pl.ANY)
    panel = (BLOCK, RANK)
    users = UB * BLOCK
    return pl.pallas_call(
        kernel,
        out_shape=jax.ShapeDtypeStruct((users, RANK), F32),
        in_specs=[hbm, hbm, hbm],
        out_specs=pl.BlockSpec(memory_space=pltpu.VMEM),
        scratch_shapes=[
            pltpu.VMEM((1, 128), jnp.int32), pltpu.SMEM((1, 128), jnp.int32),
            pltpu.VMEM((PANELS_DEV, *panel), BF), pltpu.VMEM((UB * TP, BLOCK, BLOCK), BF),
            pltpu.VMEM((ND, *panel), BF), pltpu.VMEM((NC, NY, NX, 8, RANK), F32),
            pltpu.VMEM((PANELS_DEV, *panel), BF), pltpu.VMEM((PANELS_DEV, *panel), BF),
            pltpu.VMEM((PANELS_DEV, *panel), BF),
            pltpu.VMEM((3, 1, 128), jnp.int32), pltpu.SMEM((3, 1, 128), jnp.int32),
            pltpu.VMEM((NG, *panel), BF), pltpu.VMEM((NG, *panel), BF), pltpu.VMEM((NG, *panel), BF),
            pltpu.VMEM((NG, *panel), BF), pltpu.VMEM((4, NG, *panel), BF),
            pltpu.VMEM((len(NEAR), *panel), BF), pltpu.VMEM((3, NX - 1, *panel), BF),
            pltpu.VMEM((RANK, RANK), F32), pltpu.VMEM((128, RANK), F32),
            pltpu.VMEM((NY, 32, RANK), F32), pltpu.VMEM((NY, 32, RANK), F32),
            pltpu.VMEM((NX, 8, RANK), F32), pltpu.VMEM((NX, 8, RANK), F32),
            pltpu.VMEM((8, RANK), F32), pltpu.VMEM((NZ, 8, RANK), F32), pltpu.VMEM((NX, 8, RANK), F32),
            pltpu.VMEM((UB * TP * BLOCK, RANK), BF), pltpu.VMEM((UB * TP * BLOCK, RANK), BF),
            pltpu.VMEM((RANK, RANK), BF), pltpu.VMEM((RANK, RANK), BF),
            pltpu.VMEM((users, RANK), F32), pltpu.VMEM((users, RANK), F32), pltpu.VMEM((users, 128), F32),
            dma((4,)),
            dma((3,)), dma((3,)), dma((3,)),
            dma((4,)), dma((4,)),
            dma((4, NG)), dma((4, NG)),
            dma((len(NEAR),)), dma((ND,)), dma((3, NX - 1)),
            dma((1,)), dma((1,)), dma((NY,)), dma((NY,)), dma((NX,)), dma((NX,)), dma((NZ,)), dma((NZ,)),
            dma((NX,)), dma((NX,)), dma((NY,)), dma((NY,)), dma((1,)), dma((1,)),
        ],
        name="half_sweep",
        compiler_params=pltpu.CompilerParams(collective_id=0, has_side_effects=True, vmem_limit_bytes=60 * 1024 * 1024),
    )(meta, items, conf)


def shards(item_factors, send_list, route_list, tile_slot, confidence):
    meta = jnp.concatenate(
        [send_list.reshape(1, -1), route_list.reshape(1, -1), tile_slot, jnp.zeros((1, 24), jnp.int32)], axis=1
    )
    return half_sweep(meta, item_factors.reshape(-1, BLOCK, RANK), confidence)


def solution(mesh):
    placed = (
        P(("grp", "dev"), None),
        P(("grp", "dev"), None, None),
        P(("grp", "dev"), None, None),
        P(("grp", "dev"), None),
        P(("grp", "dev"), None, None),
    )
    return jax.shard_map(
        shards, mesh=mesh, in_specs=placed, out_specs=P(("grp", "dev"), None), check_vma=False
    )
```

time: 423 us -> 74.7 us (0.18)
  waiting for transfers between devices: 249 us -> 0 us
  matrix products: 72.9 us -> 0 us
  Pallas kernels: 0 us -> 71.4 us
  blocking collectives: 52.4 us -> 0 us
  local copies, waits for them, and re-layouts: 17.8 us -> 1.87 us
  between operations: 15.1 us -> 0.01 us
  other arithmetic: 14.6 us -> 1.27 us
    psum x1 -> x0, waiting for transfers between devices: 153 us -> none  [shards(): gram = lax.psum(partial_gram, ('grp', 'dev'))]
    all_gather x1 -> x0, waiting for transfers between devices: 95.5 us -> none  [shards(): everyone = lax.all_gather(group_pool, 'dev', axis=0, tiled=True)]
    dot_general x18 -> x0, matrix products: 72.9 us -> none  [the longest x8 55.9 us: apply_operator(): jnp.einsum('utbi,utir->ubr', weighted, tile_panels, preferred_element_typ...]
    pallas_call x0 -> x1, Pallas kernels: none -> 71.4 us  [half_sweep(): pl.pallas_call(kernel, out_shape=jax.ShapeDtypeStruct((users, RANK), F32)...]
    all_gather x1 -> x0, blocking collectives: 36.8 us -> none  [shards(): all_routes = lax.all_gather(route_list, 'dev', axis=0, tiled=True)]
    all_to_all x1 -> x0, blocking collectives: 15.6 us -> none  [shards(): lax.all_to_all(outgoing, 'grp', split_axis=0, concat_axis=0, tiled=True)]
    gather x3 -> x0, local copies, waits for them, and re-layouts: 9.8 us -> none  [the longest x1 6.48 us: shards(): panels = everyone[(sources + mine).reshape(-1)]]
    convert_element_type x7 -> x0, other arithmetic: 7.09 us -> none  [apply_operator(): dir_bf = direction.astype(jnp.bfloat16).reshape(USER_BLOCKS, BLOCK, RANK)]
  transfers between devices with their start and end apart: 2 -> 0, of which waited for: 2 -> 0; matrix products, arithmetic and copies ran while one was open for 7% -> 0% of each run, Pallas kernels for 0% -> 0%
where the time goes in v2:
time: 74.7 us; the launch traced here: 74.6 us
  Pallas kernels  71.4 us (96%)
  local copies, waits for them, and re-layouts  1.87 us (3%)
  other arithmetic  1.27 us (2%)
    pallas_call x1, Pallas kernels, half_sweep(): pl.pallas_call(kernel, out_shape=jax.ShapeDtypeStruct((users, RANK), F32)...  71.4 us
    unnamed x1, local copies, waits for them, and re-layouts  1.87 us

profile of v2, /device:TPU:1, one launch (start us, length us, event | category | flops | bytes accessed | tf_op | source)
XLA Modules:
  0.0 74.6 jit_solution(5713817521971746125)
XLA Ops:
  0.0 1.3 %bitcast_add_fusion.meta_h = s32[1,128]{1,0:T(1,128)} fusion(s32[24]{0:T(128)S(1)} %broadcast.3, s32[1,64]{1,0:T(1,128)} %param.8, s32[1,32]{1,0:T(1,128)} %bitcast.6, s32[1,8]{1,0:T(1,128)} %bitcast.7), kind=kLoop, calls=%fused_computation | loop fusion | flops 384 | bytes 1024 | tf_op jit(solution)/shard_map/concatenate | solution.py:332
  1.3 71.4 %half_sweep.1 = f32[512,256]{1,0:T(8,128)} custom-call(s32[1,128]{1,0:T(1,128)} %bitcast_add_fusion.meta_h, bf16[2,128,256]{2,1,0:T(8,128)(2,1)} %bitcast.5, bf16[64,128,128]{2,1,0:T(8,128)(2,1)} %conf_h.1), custom_call_target="tpu_custom_call" | custom-call | tf_op jit(solution)/shard_map/half_sweep/pallas_call | solution.py:296
  72.7 1.9 %copy.7 = f32[512,256]{1,0:T(8,128)} copy(f32[512,256]{1,0:T(8,128)} %half_sweep.1) | data formatting | bytes 1048576
  (1 shorter events, 0.0 us)

commit v3 on v2

--- a/solution.py
+++ b/solution.py
@@ -16,13 +16,12 @@
 RIDGE = 0.1
 NG, NY, NC, NX, NZ = 8, 4, 2, 4, 8
 ND = NX * NZ
-SEND_AT, ROUTE_AT, SLOT_AT = 0, 8, 40
 F32 = jnp.float32
 BF = jnp.bfloat16
 MESH = pl.DeviceIdType.MESH
 FAR = (3, 5, 4)
 NEAR = tuple((dz, dx) for dz in (2, 6, 1, 7, 0) for dx in (2, 1, 3, 0) if (dz, dx) != (0, 0))
-FIRST = 10
+FIRST = 0
 CHUNK = 1024
 
 
@@ -38,7 +37,7 @@
     tiles = UB * TP
 
     def gather(t, carry):
-        pan[pl.ds(pl.multiple_of(t * BLOCK, BLOCK), BLOCK), :] = slots[meta[0, SLOT_AT + t]]
+        pan[pl.ds(pl.multiple_of(t * BLOCK, BLOCK), BLOCK), :] = slots[meta[0, t]]
         return carry
 
     lax.fori_loop(0, tiles, gather, 0, unroll=4)
@@ -100,7 +99,7 @@
     lax.fori_loop(0, ITERS, step, 0)
 
 
-def exchange(meta_v, meta, items, slots, gram, raw, metas_v, metas, pools, out1, out2, out3, part,
+def exchange(send_v, route_v, send_s, route_s, items, slots, gram, raw, sends_v, routes_v, sends_s, routes_s, pools, out1, out2, out3, part,
              gc, sc, gy, s2, g2, s3, g3, s4, local, sm, rm, sr, rr, sp, rp, sn, rs, sx,
              cs, cr, ys, yr, xs, xr, zs, zr, as_, ar, bs, br, es, er, before_wait):
     g = lax.axis_index("grp")
@@ -150,12 +149,13 @@
     flat = items[...].reshape(PANELS_DEV * BLOCK, RANK)
     part[...] = lax.dot_general(flat, flat, (((0,), (0,)), ((), ())), preferred_element_type=F32)
     for j in range(NG):
-        out1[3, j] = items[meta[0, SEND_AT + j]]
+        out1[3, j] = items[send_s[0, j]]
     pools[3][g] = out1[3, g]
     pl.semaphore_wait(barrier, len(grp_peers) + len(near) + len(FAR))
 
     for i, o in enumerate(FAR):
-        send(meta_v, metas_v.at[i], sm.at[i], rm.at[i], at_z(NZ - o))
+        send(send_v, sends_v.at[i], sm.at[0, i], rm.at[0, i], at_z(NZ - o))
+        send(route_v, routes_v.at[i], sm.at[1, i], rm.at[1, i], at_z(NZ - o))
     for i in range(2):
         send(items, raw[i], sr.at[i], rr.at[i], at_z(NZ - FAR[i]))
     for p in grp_peers:
@@ -173,7 +173,7 @@
 
     def fill(n):
         if n < len(near):
-            out2[n] = pools[3][meta[0, ROUTE_AT + near[n]]]
+            out2[n] = pools[3][route_s[0, near[n]]]
 
     def ship(n):
         send(out2.at[n], slots.at[d], sn.at[n], rs.at[d], {"dev": near[n]})
@@ -193,16 +193,19 @@
 
     def proxy(i):
         for j in range(NG):
-            out1[i, j] = raw[i][metas[i, 0, SEND_AT + j]]
+            out1[i, j] = raw[i][sends_s[i, 0, j]]
         pools[i][g] = out1[i, g]
         for p in grp_peers:
             send(out1.at[i, p], pools[i].at[g], sp.at[i, p], rp.at[i, g], {"grp": p})
 
     for i in range(3):
-        arrived(metas_v.at[i], sm.at[i], rm.at[i])
-        pltpu.make_async_copy(metas_v.at[i], metas.at[i], local.at[i]).start()
+        arrived(sends_v.at[i], sm.at[0, i], rm.at[0, i])
+        pltpu.make_async_copy(sends_v.at[i], sends_s.at[i], local.at[0, i]).start()
+        arrived(routes_v.at[i], sm.at[1, i], rm.at[1, i])
+        pltpu.make_async_copy(routes_v.at[i], routes_s.at[i], local.at[1, i]).start()
     for i in range(3):
-        pltpu.make_async_copy(metas_v.at[i], metas.at[i], local.at[i]).wait()
+        pltpu.make_async_copy(sends_v.at[i], sends_s.at[i], local.at[0, i]).wait()
+        pltpu.make_async_copy(routes_v.at[i], routes_s.at[i], local.at[1, i]).wait()
     arrived(raw[0], sr.at[0], rr.at[0])
     send(raw[0].at[1], raw[2].at[1], sr.at[3], rr.at[3], at_z(NZ - 1))
     arrived(raw[1], sr.at[1], rr.at[1])
@@ -236,12 +239,12 @@
         slot = lax.rem(z + FAR[i], NZ) * NX + x
         pool_ready(i)
         for k, p in enumerate(x_peers):
-            out3[i, k] = pools[i][metas[i, 0, ROUTE_AT + z * NX + p]]
+            out3[i, k] = pools[i][routes_s[i, 0, z * NX + p]]
         for k, p in enumerate(x_peers):
             send(out3.at[i, k], slots.at[slot], sx.at[i, k], rs.at[slot], at_x(p))
-        slots[slot] = pools[i][metas[i, 0, ROUTE_AT + d]]
-
-    slots[d] = pools[3][meta[0, ROUTE_AT + d]]
+        slots[slot] = pools[i][routes_s[i, 0, d]]
+
+    slots[d] = pools[3][route_s[0, d]]
     relay(0)
     relay(1)
     for p in x_peers:
@@ -265,30 +268,29 @@
         copy.wait_send()
 
 
-def kernel(meta_h, items_h, conf_h, out, meta_v, meta, items, conf, slots, gram, raw0, raw1, raw2, metas_v, metas,
-           pool0, pool1, pool2, pool3, out1, out2, out3, part, gc, sc, gy, s2, g2, s3, g3, s4, pan, pant, gh, gl, res, dirn, rr, *sems):
+def kernel(send_h, route_h, slot_h, items_h, conf_h, out, send_v, route_v, send_s, route_s, slot_s, items, conf,
+           slots, gram, raw0, raw1, raw2, sends_v, routes_v, sends_s, routes_s, pool0, pool1, pool2, pool3,
+           out1, out2, out3, part, gc, sc, gy, s2, g2, s3, g3, s4, pan, pant, gh, gl, res, dirn, rr, *sems):
     ins, sems = sems[0], sems[1:]
-    loads = [
-        pltpu.make_async_copy(meta_h, meta, ins.at[0]),
-        pltpu.make_async_copy(meta_h, meta_v, ins.at[1]),
-        pltpu.make_async_copy(items_h, items, ins.at[2]),
-        pltpu.make_async_copy(conf_h, conf, ins.at[3]),
-    ]
+    pairs = ((send_h, send_s), (route_h, route_s), (items_h, items), (send_h, send_v), (route_h, route_v),
+             (slot_h, slot_s), (conf_h, conf))
+    loads = [pltpu.make_async_copy(a, b, ins.at[i]) for i, (a, b) in enumerate(pairs)]
     for copy in loads:
         copy.start()
 
     def ready():
-        for copy in loads[:3]:
+        for copy in loads[:5]:
             copy.wait()
 
-    exchange(meta_v, meta, items, slots, gram, (raw0, raw1, raw2), metas_v, metas,
-             (pool0, pool1, pool2, pool3), out1, out2, out3, part,
+    exchange(send_v, route_v, send_s, route_s, items, slots, gram, (raw0, raw1, raw2), sends_v, routes_v,
+             sends_s, routes_s, (pool0, pool1, pool2, pool3), out1, out2, out3, part,
              gc, sc, gy, s2, g2, s3, g3, s4, *sems, ready)
-    loads[3].wait()
-    solve(meta, slots, gram, conf, out, pan, pant, gh, gl, res, dirn, rr)
-
-
-def half_sweep(meta, items, conf):
+    loads[5].wait()
+    loads[6].wait()
+    solve(slot_s, slots, gram, conf, out, pan, pant, gh, gl, res, dirn, rr)
+
+
+def half_sweep(send_list, route_list, tile_slot, items, conf):
     dma = pltpu.SemaphoreType.DMA
     hbm = pl.BlockSpec(memory_space=pl.ANY)
     panel = (BLOCK, RANK)
@@ -296,15 +298,17 @@
     return pl.pallas_call(
         kernel,
         out_shape=jax.ShapeDtypeStruct((users, RANK), F32),
-        in_specs=[hbm, hbm, hbm],
+        in_specs=[hbm] * 5,
         out_specs=pl.BlockSpec(memory_space=pltpu.VMEM),
         scratch_shapes=[
-            pltpu.VMEM((1, 128), jnp.int32), pltpu.SMEM((1, 128), jnp.int32),
+            pltpu.VMEM((1, NG), jnp.int32), pltpu.VMEM((1, ND), jnp.int32),
+            pltpu.SMEM((1, NG), jnp.int32), pltpu.SMEM((1, ND), jnp.int32), pltpu.SMEM((1, UB * TP), jnp.int32),
             pltpu.VMEM((PANELS_DEV, *panel), BF), pltpu.VMEM((UB * TP, BLOCK, BLOCK), BF),
             pltpu.VMEM((ND, *panel), BF), pltpu.VMEM((NC, NY, NX, 8, RANK), F32),
             pltpu.VMEM((PANELS_DEV, *panel), BF), pltpu.VMEM((PANELS_DEV, *panel), BF),
             pltpu.VMEM((PANELS_DEV, *panel), BF),
-            pltpu.VMEM((3, 1, 128), jnp.int32), pltpu.SMEM((3, 1, 128), jnp.int32),
+            pltpu.VMEM((3, 1, NG), jnp.int32), pltpu.VMEM((3, 1, ND), jnp.int32),
+            pltpu.SMEM((3, 1, NG), jnp.int32), pltpu.SMEM((3, 1, ND), jnp.int32),
             pltpu.VMEM((NG, *panel), BF), pltpu.VMEM((NG, *panel), BF), pltpu.VMEM((NG, *panel), BF),
             pltpu.VMEM((NG, *panel), BF), pltpu.VMEM((4, NG, *panel), BF),
             pltpu.VMEM((len(NEAR), *panel), BF), pltpu.VMEM((3, NX - 1, *panel), BF),
@@ -315,8 +319,8 @@
             pltpu.VMEM((UB * TP * BLOCK, RANK), BF), pltpu.VMEM((UB * TP * BLOCK, RANK), BF),
             pltpu.VMEM((RANK, RANK), BF), pltpu.VMEM((RANK, RANK), BF),
             pltpu.VMEM((users, RANK), F32), pltpu.VMEM((users, RANK), F32), pltpu.VMEM((users, 128), F32),
-            dma((4,)),
-            dma((3,)), dma((3,)), dma((3,)),
+            dma((7,)),
+            dma((2, 3)), dma((2, 3)), dma((2, 3)),
             dma((4,)), dma((4,)),
             dma((4, NG)), dma((4, NG)),
             dma((len(NEAR),)), dma((ND,)), dma((3, NX - 1)),
@@ -324,15 +328,15 @@
             dma((NX,)), dma((NX,)), dma((NY,)), dma((NY,)), dma((1,)), dma((1,)),
         ],
         name="half_sweep",
-        compiler_params=pltpu.CompilerParams(collective_id=0, has_side_effects=True, vmem_limit_bytes=60 * 1024 * 1024),
-    )(meta, items, conf)
+        compiler_params=pltpu.CompilerParams(collective_id=0, has_side_effects=True, vmem_limit_bytes=54000 << 10),
+    )(*[pltpu.with_memory_space_constraint(a, pltpu.HBM) for a in (send_list, route_list, tile_slot, items, conf)])
 
 
 def shards(item_factors, send_list, route_list, tile_slot, confidence):
-    meta = jnp.concatenate(
-        [send_list.reshape(1, -1), route_list.reshape(1, -1), tile_slot, jnp.zeros((1, 24), jnp.int32)], axis=1
+    return half_sweep(
+        send_list.reshape(1, -1), route_list.reshape(1, -1), tile_slot,
+        item_factors.reshape(-1, BLOCK, RANK), confidence,
     )
-    return half_sweep(meta, item_factors.reshape(-1, BLOCK, RANK), confidence)
 
 
 def solution(mesh):

time: 74.7 us -> 70.6 us (0.945)
  Pallas kernels: 71.4 us -> 69.8 us
  other arithmetic: 1.27 us -> 0 us
  local copies, waits for them, and re-layouts: 1.87 us -> 0.8 us
    pallas_call x1, Pallas kernels: 71.4 us -> 69.8 us  [half_sweep(): pl.pallas_call(kernel, out_shape=jax.ShapeDtypeStruct((users, RANK), F32)...]
    concatenate x1 -> x0, other arithmetic: 1.27 us -> none  [shards(): jnp.concatenate([send_list.reshape(1, -1), route_list.reshape(1, -1), til...]
    unnamed x1, local copies, waits for them, and re-layouts: 1.87 us -> 0.8 us
where the time goes in v3:
time: 70.6 us
  Pallas kernels  69.8 us (99%)
  local copies, waits for them, and re-layouts  0.8 us (1%)
    pallas_call x1, Pallas kernels, half_sweep(): pl.pallas_call(kernel, out_shape=jax.ShapeDtypeStruct((users, RANK), F32)...  69.8 us

profile of v3, /device:TPU:1, one launch (start us, length us, event | category | flops | bytes accessed | tf_op | source)
XLA Modules:
  0.0 70.6 jit_solution(4153594393215283540)
XLA Ops:
  0.0 69.8 %half_sweep.1 = f32[512,256]{1,0:T(8,128)S(1)} custom-call(s32[1,8]{1,0:T(1,128)} %bitcast.4, s32[1,32]{1,0:T(1,128)} %bitcast.5, s32[1,64]{1,0:T(1,128)} %slot_h.1, bf16[2,128,256]{2,1,0:T(8,128)(2,1)} %bitcast.3, bf16[64,128,128]{2,1,0:T(8,128)(2,1)} %conf_h.1), custom_call_target="tpu_custom_call" | custom-call | tf_op jit(solution)/shard_map/half_sweep/pallas_call | solution.py:298
  69.8 0.8 %copy.7 = f32[512,256]{1,0:T(8,128)} copy(f32[512,256]{1,0:T(8,128)S(1)} %half_sweep.1) | data formatting | bytes 1048576

commit v4 on v3

v4 whole, which is shorter than its diff:
```python
import functools

import jax
import jax.numpy as jnp
from jax import lax
from jax.experimental import pallas as pl
from jax.experimental.pallas import tpu as pltpu
from jax.sharding import PartitionSpec as P

PANELS_DEV = 2
RANK = 256
BLOCK = 128
UB = 4
TP = 16
ITERS = 8
RIDGE = 0.1
NG, NY, NC, NX, NZ = 8, 4, 2, 4, 8
ND = NX * NZ
F32 = jnp.float32
BF = jnp.bfloat16
MESH = pl.DeviceIdType.MESH
FAR = (3, 5, 4)
NEAR = tuple((dz, dx) for dz in (2, 6, 1, 7, 0) for dx in (2, 1, 3, 0) if (dz, dx) != (0, 0))
NH = 1
HB = BLOCK // NH
PLAN = ("X", "P", "Y", "R", 19, "F", "Z", "L", "A", "M")
CHUNK = 1024
PER = CHUNK // BLOCK
WIDE = True


def dot(a, b):
    return jnp.dot(a, b, preferred_element_type=F32)


def half(ref, i):
    return ref.at[pl.ds(pl.multiple_of(i * 128, 128), 128), :]


def confs(conf, b, c):
    return jnp.concatenate([conf[b * TP + c * PER + j] for j in range(PER)], axis=1).astype(F32)


def chunk(b, c):
    first = (b * TP + c * PER) * BLOCK
    return slice(first, first + CHUNK)


def gather_panels(slot_s, slots, pan, pant):
    def gather(t, carry):
        pan[pl.ds(pl.multiple_of(t * BLOCK, BLOCK), BLOCK), :] = slots[slot_s[0, t]]
        return carry

    lax.fori_loop(0, UB * TP, gather, 0, unroll=4)

    def turn(q, carry):
        rows = pl.ds(pl.multiple_of(q * 256, 256), 256)
        pant[rows, :] = pan[rows, :].T
        return carry

    lax.fori_loop(0, UB * TP // 2, turn, 0)


def right_side(conf, out, pan, res, dirn, rr):
    for b in range(UB):
        acc = None
        for c in range(TP // PER):
            w = confs(conf, b, c)
            d = dot(jnp.where(w > 0, 1.0 + w, 0.0).astype(BF), pan[chunk(b, c), :])
            acc = d if acc is None else acc + d
        us = slice(b * BLOCK, (b + 1) * BLOCK)
        res[us, :] = acc
        dirn[us, :] = acc
        out[us, :] = jnp.zeros_like(acc)
        rr[us, :] = jnp.broadcast_to(jnp.sum(acc * acc, axis=1, keepdims=True), (BLOCK, 128))


def solve(gram, conf, out, pan, pant, gh, gl, res, dirn, rr, gv):
    g = gram[...].reshape(RANK, RANK)
    high = g.astype(BF)
    gh[...] = high
    gl[...] = (g - high.astype(F32)).astype(BF)

    def step(i, carry):
        if WIDE:
            v = dirn[...]
            vb = v.astype(BF)
            vl = (v - vb.astype(F32)).astype(BF)
            gv[...] = dot(vb, gh[...]) + dot(vb, gl[...])
        for b in range(UB):
            us = slice(b * BLOCK, (b + 1) * BLOCK)
            v = dirn[us, :]
            vb = v.astype(BF)
            if WIDE:
                acc = gv[us, :] + RIDGE * v
            else:
                vl = (v - vb.astype(F32)).astype(BF)
                acc = dot(vb, gh[...]) + dot(vb, gl[...]) + dot(vl, gh[...]) + RIDGE * v
            for c in range(TP // PER):
                first = (b * TP + c * PER) * BLOCK
                s = jnp.concatenate(
                    [dot(vb, pant[first + 256 * j : first + 256 * j + 256, :]) for j in range(PER // 2)], axis=1
                )
                acc = acc + dot((confs(conf, b, c) * s).astype(BF), pan[chunk(b, c), :])
            old = rr[us, 0:1]
            alpha = old / jnp.sum(v * acc, axis=1, keepdims=True)
            out[us, :] = out[us, :] + alpha * v
            r = res[us, :] - alpha * acc
            new = jnp.sum(r * r, axis=1, keepdims=True)
            res[us, :] = r
            dirn[us, :] = r + (new / old) * v
            rr[us, :] = jnp.broadcast_to(new, (BLOCK, 128))
        return carry

    lax.fori_loop(0, ITERS, step, 0)


def exchange(send_v, route_v, send_s, route_s, items, slots, gram, raw, sends_v, routes_v, sends_s, routes_s,
             pool, pools, out1, out2, out3, out4, part, gc, sc, gx, s2, g2, s3, g3, s4,
             local, sm, rm, sr, rr, sp, rp, sq, rq, sn, rs, sx,
             cs, cr, ys, yr, xs, xr, zs, zr, as_, ar, bs, br, es, er, before_wait):
    g = lax.axis_index("grp")
    d = lax.axis_index("dev")
    z, x = d // NX, lax.rem(d, NX)
    y, c = g // NC, lax.rem(g, NC)
    grp_peers = [lax.rem(g + k, NG) for k in (1, 3, 5, 7, 2, 6, 4)]
    x_peers = [lax.rem(x + k, NX) for k in range(1, NX)]
    y_peers = [lax.rem(y + k, NY) for k in range(1, NY)]
    z_peers = [lax.rem(z + k, NZ) for k in range(1, NZ)]

    def at_z(k):
        return {"dev": lax.rem(z + k, NZ) * NX + x}

    def at_x(p):
        return {"dev": z * NX + p}

    def at_y(p):
        return {"grp": p * NC + c}

    other = {"grp": y * NC + 1 - c}

    barrier = pltpu.get_barrier_semaphore()
    near = [lax.rem(z + dz, NZ) * NX + lax.rem(x + dx, NX) for dz, dx in NEAR]
    for p in grp_peers:
        pl.semaphore_signal(barrier, inc=1, device_id={"grp": p}, device_id_type=MESH)
    for e in near:
        pl.semaphore_signal(barrier, inc=1, device_id={"dev": e}, device_id_type=MESH)
    for o in FAR:
        pl.semaphore_signal(barrier, inc=1, device_id=at_z(o), device_id_type=MESH)

    started = []

    def send(src, dst, ss, rs_, where):
        copy = pltpu.make_async_remote_copy(
            src_ref=src, dst_ref=dst, send_sem=ss, recv_sem=rs_, device_id=where, device_id_type=MESH
        )
        copy.start()
        started.append(copy)

    def arrived(ref, ss, rs_):
        pltpu.make_async_remote_copy(
            src_ref=ref, dst_ref=ref, send_sem=ss, recv_sem=rs_, device_id=other, device_id_type=MESH
        ).wait_recv()

    before_wait()
    flat = items[...].reshape(PANELS_DEV * BLOCK, RANK)
    part[...] = lax.dot_general(flat, flat, (((0,), (0,)), ((), ())), preferred_element_type=F32)
    for j in range(NG):
        out1[j] = items[send_s[0, j]]
    pool[g] = out1[g]
    pl.semaphore_wait(barrier, len(grp_peers) + len(near) + len(FAR))

    for i, o in enumerate(FAR):
        send(send_v, sends_v.at[i], sm.at[0, i], rm.at[0, i], at_z(NZ - o))
        send(route_v, routes_v.at[i], sm.at[1, i], rm.at[1, i], at_z(NZ - o))
    def rows(h):
        return slice(h * HB, h * HB + HB)

    def send_raw(h):
        for i in range(2):
            send(items.at[:, rows(h), :], raw[i][h], sr.at[h, i], rr.at[h, i], at_z(NZ - FAR[i]))

    send_raw(0)
    for p in grp_peers:
        send(out1.at[p], pool.at[g], sp.at[p], rp.at[g], {"grp": p})
    for h in range(1, NH):
        send_raw(h)
    send(half(part, 1 - c), gc, cs.at[0], cr.at[0], other)
    arrived(gc, cs.at[0], cr.at[0])
    sc[...] = (half(part, c)[...] + gc[...]).reshape(NX, 32, RANK)
    gx[x] = sc[x]
    for p in x_peers:
        send(sc.at[p], gx.at[x], xs.at[p], xr.at[x], at_x(p))

    def fill(n):
        if n < len(near):
            out2[n] = pool[route_s[0, near[n]]]

    def ship(first, last):
        for n in range(first, last):
            fill(n + 2)
            send(out2.at[n], slots.at[d], sn.at[n], rs.at[0, d], {"dev": near[n]})

    def proxy(i, h):
        for j in range(NG):
            out4[i, h, j] = raw[i][h][sends_s[i, 0, j]]
        pools[i][h][g] = out4[i, h, g]
        for p in grp_peers:
            send(out4.at[i, h, p], pools[i][h].at[g], sq.at[i, h, p], rq.at[i, h, g], {"grp": p})

    for i in range(3):
        arrived(sends_v.at[i], sm.at[0, i], rm.at[0, i])
        pltpu.make_async_copy(sends_v.at[i], sends_s.at[i], local.at[0, i]).start()
        arrived(routes_v.at[i], sm.at[1, i], rm.at[1, i])
        pltpu.make_async_copy(routes_v.at[i], routes_s.at[i], local.at[1, i]).start()
    for i in range(3):
        pltpu.make_async_copy(sends_v.at[i], sends_s.at[i], local.at[0, i]).wait()
        pltpu.make_async_copy(routes_v.at[i], routes_s.at[i], local.at[1, i]).wait()

    def raw_in(h):
        arrived(raw[0][h], sr.at[h, 0], rr.at[h, 0])
        send(raw[0][h].at[1], raw[2][h].at[1], sr.at[h, 3], rr.at[h, 3], at_z(NZ - 1))
        arrived(raw[1][h], sr.at[h, 1], rr.at[h, 1])
        send(raw[1][h].at[0], raw[2][h].at[0], sr.at[h, 2], rr.at[h, 2], at_z(1))
        proxy(0, h)
        proxy(1, h)

    def relay(i, h):
        slot = lax.rem(z + FAR[i], NZ) * NX + x
        for p in grp_peers:
            arrived(pools[i][h].at[p], sq.at[i, h, p], rq.at[i, h, p])
        for k, p in enumerate(x_peers):
            out3[i, h, k] = pools[i][h][routes_s[i, 0, z * NX + p]]
        for k, p in enumerate(x_peers):
            send(out3.at[i, h, k], slots.at[slot, rows(h), :], sx.at[i, h, k], rs.at[h, slot], at_x(p))
        slots[slot, rows(h), :] = pools[i][h][routes_s[i, 0, d]]

    def pool_in():
        for p in grp_peers:
            arrived(pool.at[p], sp.at[p], rp.at[p])
        fill(0)
        fill(1)
        slots[d] = pool[route_s[0, d]]

    def gram_x():
        for p in x_peers:
            arrived(gx.at[p], xs.at[p], xr.at[p])
        s2[...] = ((gx[0] + gx[1]) + (gx[2] + gx[3])).reshape(NY, 8, RANK)
        g2[y] = s2[y]
        for p in y_peers:
            send(s2.at[p], g2.at[y], ys.at[p], yr.at[y], at_y(p))

    def gram_y():
        for p in y_peers:
            arrived(g2.at[p], ys.at[p], yr.at[p])
        s3[...] = (g2[0] + g2[1]) + (g2[2] + g2[3])
        g3[z] = s3[...]
        for k, p in enumerate(z_peers):
            send(s3, g3.at[z], zs.at[p], zr.at[z], at_z(k + 1))

    def far_in():
        for h in range(NH):
            arrived(raw[2][h].at[0], sr.at[h, 2], rr.at[h, 2])
            arrived(raw[2][h].at[1], sr.at[h, 3], rr.at[h, 3])
            proxy(2, h)

    def gram_z():
        for p in z_peers:
            arrived(g3.at[p], zs.at[p], zr.at[p])
        s4[x] = ((g3[0] + g3[1]) + (g3[2] + g3[3])) + ((g3[4] + g3[5]) + (g3[6] + g3[7]))
        for p in x_peers:
            send(s4.at[x], s4.at[x], as_.at[p], ar.at[x], at_x(p))

    def gram_back():
        for p in x_peers:
            arrived(s4.at[p], as_.at[p], ar.at[p])
        gram[c, :, y] = s4[...]
        for p in y_peers:
            send(s4, gram.at[c, :, y], bs.at[p], br.at[y], at_y(p))

    def relay_near():
        for h in range(NH):
            relay(0, h)
            relay(1, h)

    def relay_last():
        for h in range(NH):
            relay(2, h)

    steps = {"P": pool_in, "X": gram_x, "Y": gram_y, "F": far_in, "Z": gram_z, "A": gram_back,
             "R": lambda: [raw_in(h) for h in range(NH)], "L": relay_near, "M": relay_last,
             "0": lambda: relay(0, 0), "1": lambda: relay(1, 0)}
    shipped = 0
    for do in PLAN:
        if isinstance(do, int):
            ship(shipped, do)
            shipped = do
        else:
            steps[do]()

    for n, e in enumerate(near):
        arrived(slots.at[e], sn.at[n], rs.at[0, e])
    for i, o in enumerate(FAR):
        for k, p in enumerate(x_peers):
            slot = lax.rem(z + o, NZ) * NX + p
            for h in range(NH):
                arrived(slots.at[slot, rows(h), :], sx.at[i, h, k], rs.at[h, slot])

    def gather_core():
        for p in y_peers:
            arrived(gram.at[c, :, p], bs.at[p], br.at[p])
        send(gram.at[c], gram.at[c], es.at[0], er.at[0], other)

    def finish():
        arrived(gram.at[1 - c], es.at[0], er.at[0])
        for copy in started:
            copy.wait_send()

    return gather_core, finish


def kernel(send_h, route_h, slot_h, items_h, conf_h, out, send_v, route_v, send_s, route_s, slot_s, items, conf,
           slots, gram, sends_v, routes_v, sends_s, routes_s, pool, out1, out2, out3, out4, part, gc, sc, gx,
           s2, g2, s3, g3, s4, pan, pant, gh, gl, res, dirn, rr, gv, *rest):
    raw = [rest[NH * i : NH * i + NH] for i in range(3)]
    pools = [rest[NH * (3 + i) : NH * (4 + i)] for i in range(3)]
    ins, sems = rest[6 * NH], rest[6 * NH + 1 :]
    pairs = ((send_h, send_s), (route_h, route_s), (items_h, items), (send_h, send_v), (route_h, route_v),
             (slot_h, slot_s), (conf_h, conf))
    loads = [pltpu.make_async_copy(a, b, ins.at[i]) for i, (a, b) in enumerate(pairs)]
    for copy in loads:
        copy.start()

    def ready():
        for copy in loads[:5]:
            copy.wait()

    gather_core, finish = exchange(
        send_v, route_v, send_s, route_s, items, slots, gram, raw, sends_v, routes_v, sends_s, routes_s,
        pool, pools, out1, out2, out3, out4, part, gc, sc, gx, s2, g2, s3, g3, s4, *sems, ready)
    loads[5].wait()
    gather_panels(slot_s, slots, pan, pant)
    gather_core()
    loads[6].wait()
    right_side(conf, out, pan, res, dirn, rr)
    finish()
    solve(gram, conf, out, pan, pant, gh, gl, res, dirn, rr, gv)


def half_sweep(send_list, route_list, tile_slot, items, conf):
    dma = pltpu.SemaphoreType.DMA
    hbm = pl.BlockSpec(memory_space=pl.ANY)
    panel = (BLOCK, RANK)
    users = UB * BLOCK
    return pl.pallas_call(
        kernel,
        out_shape=jax.ShapeDtypeStruct((users, RANK), F32),
        in_specs=[hbm] * 5,
        out_specs=pl.BlockSpec(memory_space=pltpu.VMEM),
        scratch_shapes=[
            pltpu.VMEM((1, NG), jnp.int32), pltpu.VMEM((1, ND), jnp.int32),
            pltpu.SMEM((1, NG), jnp.int32), pltpu.SMEM((1, ND), jnp.int32), pltpu.SMEM((1, UB * TP), jnp.int32),
            pltpu.VMEM((PANELS_DEV, *panel), BF), pltpu.VMEM((UB * TP, BLOCK, BLOCK), BF),
            pltpu.VMEM((ND, *panel), BF), pltpu.VMEM((NC, NX, NY, 8, RANK), F32),
            pltpu.VMEM((3, 1, NG), jnp.int32), pltpu.VMEM((3, 1, ND), jnp.int32),
            pltpu.SMEM((3, 1, NG), jnp.int32), pltpu.SMEM((3, 1, ND), jnp.int32),
            pltpu.VMEM((NG, *panel), BF), pltpu.VMEM((NG, *panel), BF),
            pltpu.VMEM((len(NEAR), *panel), BF), pltpu.VMEM((3, NH, NX - 1, HB, RANK), BF),
            pltpu.VMEM((3, NH, NG, HB, RANK), BF),
            pltpu.VMEM((RANK, RANK), F32), pltpu.VMEM((128, RANK), F32),
            pltpu.VMEM((NY, 32, RANK), F32), pltpu.VMEM((NY, 32, RANK), F32),
            pltpu.VMEM((NX, 8, RANK), F32), pltpu.VMEM((NX, 8, RANK), F32),
            pltpu.VMEM((8, RANK), F32), pltpu.VMEM((NZ, 8, RANK), F32), pltpu.VMEM((NX, 8, RANK), F32),
            pltpu.VMEM((UB * TP * BLOCK, RANK), BF), pltpu.VMEM((UB * TP * BLOCK, RANK), BF),
            pltpu.VMEM((RANK, RANK), BF), pltpu.VMEM((RANK, RANK), BF),
            pltpu.VMEM((users, RANK), F32), pltpu.VMEM((users, RANK), F32), pltpu.VMEM((users, 128), F32),
            pltpu.VMEM((users, RANK), F32),
            *[pltpu.VMEM((PANELS_DEV, HB, RANK), BF)] * (3 * NH),
            *[pltpu.VMEM((NG, HB, RANK), BF)] * (3 * NH),
            dma((7,)),
            dma((2, 3)), dma((2, 3)), dma((2, 3)),
            dma((NH, 4)), dma((NH, 4)),
            dma((NG,)), dma((NG,)), dma((3, NH, NG)), dma((3, NH, NG)),
            dma((len(NEAR),)), dma((NH, ND)), dma((3, NH, NX - 1)),
            dma((1,)), dma((1,)), dma((NY,)), dma((NY,)), dma((NX,)), dma((NX,)), dma((NZ,)), dma((NZ,)),
            dma((NX,)), dma((NX,)), dma((NY,)), dma((NY,)), dma((1,)), dma((1,)),
        ],
        name="half_sweep",
        compiler_params=pltpu.CompilerParams(collective_id=0, has_side_effects=True, vmem_limit_bytes=54000 << 10),
    )(*[pltpu.with_memory_space_constraint(a, pltpu.HBM) for a in (send_list, route_list, tile_slot, items, conf)])


def shards(item_factors, send_list, route_list, tile_slot, confidence):
    return half_sweep(
        send_list.reshape(1, -1), route_list.reshape(1, -1), tile_slot,
        item_factors.reshape(-1, BLOCK, RANK), confidence,
    )


def solution(mesh):
    placed = (
        P(("grp", "dev"), None),
        P(("grp", "dev"), None, None),
        P(("grp", "dev"), None, None),
        P(("grp", "dev"), None),
        P(("grp", "dev"), None, None),
    )
    return jax.shard_map(
        shards, mesh=mesh, in_specs=placed, out_specs=P(("grp", "dev"), None), check_vma=False
    )
```

time: 70.6 us -> 69.5 us (0.984)
  Pallas kernels: 69.8 us -> 68.6 us
    pallas_call x1, Pallas kernels: 69.8 us -> 68.6 us  [half_sweep(): pl.pallas_call(kernel, out_shape=jax.ShapeDtypeStruct((users, RANK), F32)...]
where the time goes in v4:
time: 69.5 us
  Pallas kernels  68.6 us (99%)
  local copies, waits for them, and re-layouts  0.8 us (1%)
    pallas_call x1, Pallas kernels, half_sweep(): pl.pallas_call(kernel, out_shape=jax.ShapeDtypeStruct((users, RANK), F32)...  68.6 us

profile of v4, /device:TPU:1, one launch (start us, length us, event | category | flops | bytes accessed | tf_op | source)
XLA Modules:
  0.0 69.5 jit_solution(16446281066093667421)
XLA Ops:
  0.0 68.6 %half_sweep.1 = f32[512,256]{1,0:T(8,128)S(1)} custom-call(s32[1,8]{1,0:T(1,128)} %bitcast.4, s32[1,32]{1,0:T(1,128)} %bitcast.5, s32[1,64]{1,0:T(1,128)} %slot_h.1, bf16[2,128,256]{2,1,0:T(8,128)(2,1)} %bitcast.3, bf16[64,128,128]{2,1,0:T(8,128)(2,1)} %conf_h.1), custom_call_target="tpu_custom_call" | custom-call | tf_op jit(solution)/shard_map/half_sweep/pallas_call | solution.py:355
  68.7 0.8 %copy.7 = f32[512,256]{1,0:T(8,128)} copy(f32[512,256]{1,0:T(8,128)S(1)} %half_sweep.1) | data formatting | bytes 1048576

commit v5 on v4

--- a/solution.py
+++ b/solution.py
@@ -46,19 +46,15 @@
     return slice(first, first + CHUNK)
 
 
-def gather_panels(slot_s, slots, pan, pant):
+def gather_panels(slot_s, slots, turned, pan, pant):
     def gather(t, carry):
-        pan[pl.ds(pl.multiple_of(t * BLOCK, BLOCK), BLOCK), :] = slots[slot_s[0, t]]
+        for k in range(2):
+            slot = slot_s[0, 2 * t + k]
+            pan[pl.ds(pl.multiple_of(t * RANK + k * BLOCK, BLOCK), BLOCK), :] = slots[slot]
+            pant[pl.ds(pl.multiple_of(t * RANK, RANK), RANK), k * BLOCK : k * BLOCK + BLOCK] = turned[slot]
         return carry
 
-    lax.fori_loop(0, UB * TP, gather, 0, unroll=4)
-
-    def turn(q, carry):
-        rows = pl.ds(pl.multiple_of(q * 256, 256), 256)
-        pant[rows, :] = pan[rows, :].T
-        return carry
-
-    lax.fori_loop(0, UB * TP // 2, turn, 0)
+    lax.fori_loop(0, UB * TP // 2, gather, 0, unroll=2)
 
 
 def right_side(conf, out, pan, res, dirn, rr):
@@ -115,7 +111,7 @@
     lax.fori_loop(0, ITERS, step, 0)
 
 
-def exchange(send_v, route_v, send_s, route_s, items, slots, gram, raw, sends_v, routes_v, sends_s, routes_s,
+def exchange(send_v, route_v, send_s, route_s, items, slots, turned, gram, raw, sends_v, routes_v, sends_s, routes_s,
              pool, pools, out1, out2, out3, out4, part, gc, sc, gx, s2, g2, s3, g3, s4,
              local, sm, rm, sr, rr, sp, rp, sq, rq, sn, rs, sx,
              cs, cr, ys, yr, xs, xr, zs, zr, as_, ar, bs, br, es, er, before_wait):
@@ -300,11 +296,16 @@
 
     for n, e in enumerate(near):
         arrived(slots.at[e], sn.at[n], rs.at[0, e])
+        turned[e] = slots[e].T
+    turned[d] = slots[d].T
     for i, o in enumerate(FAR):
         for k, p in enumerate(x_peers):
             slot = lax.rem(z + o, NZ) * NX + p
             for h in range(NH):
                 arrived(slots.at[slot, rows(h), :], sx.at[i, h, k], rs.at[h, slot])
+            turned[slot] = slots[slot].T
+        slot = lax.rem(z + o, NZ) * NX + x
+        turned[slot] = slots[slot].T
 
     def gather_core():
         for p in y_peers:
@@ -320,7 +321,7 @@
 
 
 def kernel(send_h, route_h, slot_h, items_h, conf_h, out, send_v, route_v, send_s, route_s, slot_s, items, conf,
-           slots, gram, sends_v, routes_v, sends_s, routes_s, pool, out1, out2, out3, out4, part, gc, sc, gx,
+           slots, turned, gram, sends_v, routes_v, sends_s, routes_s, pool, out1, out2, out3, out4, part, gc, sc, gx,
            s2, g2, s3, g3, s4, pan, pant, gh, gl, res, dirn, rr, gv, *rest):
     raw = [rest[NH * i : NH * i + NH] for i in range(3)]
     pools = [rest[NH * (3 + i) : NH * (4 + i)] for i in range(3)]
@@ -336,10 +337,10 @@
             copy.wait()
 
     gather_core, finish = exchange(
-        send_v, route_v, send_s, route_s, items, slots, gram, raw, sends_v, routes_v, sends_s, routes_s,
+        send_v, route_v, send_s, route_s, items, slots, turned, gram, raw, sends_v, routes_v, sends_s, routes_s,
         pool, pools, out1, out2, out3, out4, part, gc, sc, gx, s2, g2, s3, g3, s4, *sems, ready)
     loads[5].wait()
-    gather_panels(slot_s, slots, pan, pant)
+    gather_panels(slot_s, slots, turned, pan, pant)
     gather_core()
     loads[6].wait()
     right_side(conf, out, pan, res, dirn, rr)
@@ -361,7 +362,7 @@
             pltpu.VMEM((1, NG), jnp.int32), pltpu.VMEM((1, ND), jnp.int32),
             pltpu.SMEM((1, NG), jnp.int32), pltpu.SMEM((1, ND), jnp.int32), pltpu.SMEM((1, UB * TP), jnp.int32),
             pltpu.VMEM((PANELS_DEV, *panel), BF), pltpu.VMEM((UB * TP, BLOCK, BLOCK), BF),
-            pltpu.VMEM((ND, *panel), BF), pltpu.VMEM((NC, NX, NY, 8, RANK), F32),
+            pltpu.VMEM((ND, *panel), BF), pltpu.VMEM((ND, RANK, BLOCK), BF), pltpu.VMEM((NC, NX, NY, 8, RANK), F32),
             pltpu.VMEM((3, 1, NG), jnp.int32), pltpu.VMEM((3, 1, ND), jnp.int32),
             pltpu.SMEM((3, 1, NG), jnp.int32), pltpu.SMEM((3, 1, ND), jnp.int32),
             pltpu.VMEM((NG, *panel), BF), pltpu.VMEM((NG, *panel), BF),

time: 69.5 us -> 67.6 us (0.973)
  Pallas kernels: 68.6 us -> 66.7 us
    pallas_call x1, Pallas kernels: 68.6 us -> 66.7 us  [half_sweep(): pl.pallas_call(kernel, out_shape=jax.ShapeDtypeStruct((users, RANK), F32)...]
where the time goes in v5:
time: 67.6 us; the launch traced here: 67.5 us
  Pallas kernels  66.7 us (99%)
  local copies, waits for them, and re-layouts  0.8 us (1%)
    pallas_call x1, Pallas kernels, half_sweep(): pl.pallas_call(kernel, out_shape=jax.ShapeDtypeStruct((users, RANK), F32)...  66.7 us

profile of v5, /device:TPU:1, one launch (start us, length us, event | category | flops | bytes accessed | tf_op | source)
XLA Modules:
  0.0 67.5 jit_solution(4258010432041927346)
XLA Ops:
  0.0 66.7 %half_sweep.1 = f32[512,256]{1,0:T(8,128)S(1)} custom-call(s32[1,8]{1,0:T(1,128)} %bitcast.4, s32[1,32]{1,0:T(1,128)} %bitcast.5, s32[1,64]{1,0:T(1,128)} %slot_h.1, bf16[2,128,256]{2,1,0:T(8,128)(2,1)} %bitcast.3, bf16[64,128,128]{2,1,0:T(8,128)(2,1)} %conf_h.1), custom_call_target="tpu_custom_call" | custom-call | tf_op jit(solution)/shard_map/half_sweep/pallas_call | solution.py:356
  66.7 0.8 %copy.7 = f32[512,256]{1,0:T(8,128)} copy(f32[512,256]{1,0:T(8,128)S(1)} %half_sweep.1) | data formatting | bytes 1048576
